TPU v7x, 256 devices: a whole 4x4x8 slice. The times are simulated.
256 devices in a mesh: chan: 64 (over z, x_hi, y), sky: 4 (over x_lo, core).
Axes of the slice: x: 4 (x_hi: 2, x_lo: 2; x = x_hi * 2 + x_lo), y: 4, z: 8, core: 2. Of those that a mesh axis runs over, the one named last changes fastest.
Arguments:
- cube: float32 [512, 1024, 512], P('sky', 'chan'), may hold values from -6 to 6
- shifts: int32 [256], P('chan'), may hold values from -12 to 12
- halfwidth: int32 [256], P('chan'), may hold values from 1 to 4
- taps: float32 [1024, 9], P('chan'), may hold values from 0.1 to 1
- beam_rows: float32 [512, 512], replicated, as said below
- beam_cols: float32 [512, 512], replicated, as said below
Outputs:
- regridded: float32 [512, 1024, 512], P('sky', 'chan')
Inputs may be any that keep to these rules, and one draw needn't show every extreme that they name: beam_rows[i, j] is zero where |i - j| > 8; its diagonal exceeds the sum of the other entries of its row. beam_cols[i, j] is zero where |i - j| > 8; its diagonal exceeds the sum of the other entries of its row.
All inputs are finite; a program needn't handle non-finite values.
Results may differ from a plain program's by a relative error of at most 0.0003.
Values sent between devices are 32-bit elements; how exact they have to be, the bound alone decides.
A program may use at most 64 MiB of HBM per device.

v0:
```python
import jax
import jax.numpy as jnp
from jax import lax
from jax.sharding import PartitionSpec as P

BLK = 4
S_MAX = 12
RADIUS = 4


def with_halo(x, sides, width):
    for axis, dim in sides:
        size, length = (lax.axis_size(axis), x.shape[dim])
        up = [(i, (i + 1) % size) for i in range(size - 1)]
        down = [(j, i) for i, j in up]
        last = lax.slice_in_dim(x, length - width, length, axis=dim)
        first = lax.slice_in_dim(x, 0, width, axis=dim)
        before = lax.ppermute(last, axis, up)
        after = lax.ppermute(first, axis, down)
        x = jnp.concatenate([before, x, after], axis=dim)
    return x


def per_device(cube, shifts, halfwidth, taps, beam_rows, beam_cols):
    local_rows, chans, width = cube.shape
    reach = S_MAX + RADIUS
    taps_count = 2 * RADIUS + 1
    extended = with_halo(cube, (("chan", 1),), reach)
    chan_ids = jnp.arange(chans, dtype=jnp.int32)
    block_ids = chan_ids // BLK
    offsets = jnp.take(shifts, block_ids)
    limits = jnp.take(halfwidth, block_ids)
    tap_ids = jnp.arange(taps_count, dtype=jnp.int32)
    active = jnp.abs(tap_ids - RADIUS)[None, :] <= limits[:, None]
    masked = jnp.where(active, taps, jnp.float32(0.0))
    weights = masked / jnp.sum(masked, axis=1, keepdims=True)
    source = chan_ids[:, None] + reach + offsets[:, None] + tap_ids[None, :] - RADIUS
    positions = jnp.arange(chans + 2 * reach, dtype=jnp.int32)
    band = jnp.sum(
        jnp.where(
            source[:, :, None] == positions[None, None, :], weights[:, :, None], jnp.float32(0.0)
        ),
        axis=1,
    )
    interp = jnp.einsum("ce,hew->hcw", band, extended, precision=lax.Precision.HIGHEST)
    smoothed = jnp.einsum("hcw,vw->hcv", interp, beam_cols, precision=lax.Precision.HIGHEST)
    mixed = jnp.einsum(
        "gh,hcv->gcv",
        beam_rows,
        lax.all_to_all(smoothed, "sky", split_axis=1, concat_axis=0, tiled=True),
        precision=lax.Precision.HIGHEST,
    )
    return lax.all_to_all(mixed, "sky", split_axis=0, concat_axis=1, tiled=True)


def solution(mesh):
    placed = (P("sky", "chan", None), P("chan"), P("chan"), P("chan", None), P(), P())
    return jax.shard_map(
        per_device, mesh=mesh, in_specs=placed, out_specs=P("sky", "chan", None), check_vma=False
    )
```

profile of v0, /device:TPU:1, one launch (start us, length us, event | category | flops | bytes accessed | tf_op | source)
XLA Modules:
  0.0 256.9 jit_solution(18373305950960036583)
XLA Ops:
  0.0 0.0 copy-start
  0.0 6.1 %collective-permute-start = (f32[128,16,512]{2,1,0:T(8,128)}, f32[128,16,512]{2,1,0:T(8,128)}, u32[]{:S(2)}, u32[]{:S(2)}) collective-permute-start(f32[128,16,512]{2,1,0:T(8,128)} %param.8), channel_id=1, source_target_pairs={{0,4},{4,8},{8,12},{12,16},{16,20},{20,24},{24,28},{28,32},{32,36}... | collective-permute-start | bytes 12582920 | tf_op jit(solution)/shard_map/ppermute | solution.py:18
  6.1 1.3 collective-permute-start.1
  7.4 1.3 gather_fusion.1
  8.8 1.3 gather_fusion
  10.1 0.9 fusion.15
  11.0 0.8 fusion.14
  11.7 0.1 copy.15
  11.9 0.1 select_reduce_fusion
  12.0 81.7 %collective-permute-done = f32[128,16,512]{2,1,0:T(8,128)} collective-permute-done((f32[128,16,512]{2,1,0:T(8,128)}, f32[128,16,512]{2,1,0:T(8,128)}, u32[]{:S(2)}, u32[]{:S(2)}) %collective-permute-start) | collective-permute-done | bytes 4194336 | tf_op jit(solution)/shard_map/ppermute | solution.py:18
  93.7 5.8 %collective-permute-done.1 = f32[128,16,512]{2,1,0:T(8,128)} collective-permute-done((f32[128,16,512]{2,1,0:T(8,128)}, f32[128,16,512]{2,1,0:T(8,128)}, u32[]{:S(2)}, u32[]{:S(2)}) %collective-permute-start.1) | collective-permute-done | bytes 4194336 | tf_op jit(solution)/shard_map/ppermute | solution.py:19
  99.5 9.2 %fusion.8 = f32[128,16,512]{2,1,0:T(8,128)S(1)} fusion(f32[128,16,512]{2,1,0:T(8,128)} %collective-permute-done.1, f32[128,16,512]{2,1,0:T(8,128)} %param.8, f32[128,16,512]{2,1,0:T(8,128)} %collective-permute-done, f32[16,48]{1,0:T(8,128)S(1)} %select_reduce_fusion), kind=kOutput, calls=%fused_computation.10 | convolution fusion | flops 610271232 | bytes 16780288 | tf_op jit(solution)/shard_map/ce,hew->hcw/dot_general | solution.py:45
  108.7 0.0 copy-done
  108.7 9.3 %fusion.6 = f32[128,16,512]{2,0,1:T(8,128)S(1)} fusion(f32[128,16,512]{2,1,0:T(8,128)S(1)} %fusion.8, f32[512,512]{1,0:T(8,128)S(1)} %copy-done), kind=kOutput, calls=%fused_computation.8 | convolution fusion | flops 6442450944 | bytes 9437184 | tf_op jit(solution)/shard_map/hcw,vw->hcv/dot_general | solution.py:46
  118.0 52.3 %all_to_all.36 = f32[128,16,512]{2,0,1:T(8,128)} all-to-all(f32[128,16,512]{2,0,1:T(8,128)S(1)} %fusion.6), channel_id=1, replica_groups=mesh['chan'=64,'sky'=4] {'sky'}, dimensions={1} | all-to-all | bytes 8388608 | tf_op jit(solution)/shard_map/all_to_all | solution.py:50
  170.4 5.2 %copy.17 = f32[4,128,4,512]{1,0,3,2:T(4,128)} copy(f32[4,128,4,512]{3,1,2,0:T(8,128)} %bitcast.22) | data formatting | bytes 8388608 | tf_op jit(solution)/shard_map/all_to_all | solution.py:50
  175.6 0.0 copy-start.1
  175.6 5.6 %all_to_all.29 = f32[512,4,512]{0,2,1:T(8,128)} reshape(f32[4,128,4,512]{1,0,3,2:T(4,128)} %copy.17) | data formatting | bytes 8388608 | tf_op jit(solution)/shard_map/all_to_all | solution.py:50
  181.1 0.0 copy-done.1
  181.1 9.9 %convolution_bitcast_fusion = f32[512,4,512]{0,2,1:T(8,128)} fusion(f32[512,4,512]{0,2,1:T(8,128)} %all_to_all.29, f32[512,512]{1,0:T(8,128)S(1)} %copy-done.1), kind=kOutput, calls=%fused_computation.11 | convolution fusion | flops 6442450944 | bytes 9437184 | tf_op jit(solution)/shard_map/gh,hcv->gcv/dot_general | solution.py:47
  191.0 5.4 %copy.18 = f32[512,4,512]{2,1,0:T(4,128)} copy(f32[512,4,512]{0,2,1:T(8,128)} %convolution_bitcast_fusion) | data formatting | bytes 8388608 | tf_op jit(solution)/shard_map/gh,hcv->gcv/dot_general | solution.py:47
  196.5 51.9 %all_to_all.37 = f32[512,4,512]{2,1,0:T(4,128)S(1)} all-to-all(f32[512,4,512]{2,1,0:T(4,128)} %copy.18), channel_id=1, replica_groups=mesh['chan'=64,'sky'=4] {'sky'}, dimensions={0} | all-to-all | bytes 8388608 | tf_op jit(solution)/shard_map/all_to_all | solution.py:53
  248.4 3.3 %copy.19 = f32[128,4,4,512]{3,2,1,0:T(4,128)} copy(f32[128,4,4,512]{3,2,0,1:T(4,128)S(1)} %bitcast.23) | data formatting | bytes 8388608 | tf_op jit(solution)/shard_map/all_to_all | solution.py:53
  251.6 5.3 %all_to_all.33 = f32[128,16,512]{2,1,0:T(8,128)} reshape(f32[128,4,4,512]{3,2,1,0:T(4,128)} %copy.19) | data formatting | bytes 8388608 | tf_op jit(solution)/shard_map/all_to_all | solution.py:53
  (6 shorter events, 0.0 us)
Async XLA Ops:
  0.0 108.7 %copy-start = (f32[512,512]{1,0:T(8,128)S(1)}, f32[512,512]{1,0:T(8,128)}, u32[]{:S(2)}) copy-start(f32[512,512]{1,0:T(8,128)} %param.13) | copy-start | bytes 3145732
  0.0 93.7 %collective-permute-start = (f32[128,16,512]{2,1,0:T(8,128)}, f32[128,16,512]{2,1,0:T(8,128)}, u32[]{:S(2)}, u32[]{:S(2)}) collective-permute-start(f32[128,16,512]{2,1,0:T(8,128)} %param.8), channel_id=1, source_target_pairs={{0,4},{4,8},{8,12},{12,16},{16,20},{20,24},{24,28},{28,32},{32,36}... | collective-permute-start | bytes 12582920 | tf_op jit(solution)/shard_map/ppermute | solution.py:18
  6.1 93.4 %collective-permute-start.1 = (f32[128,16,512]{2,1,0:T(8,128)}, f32[128,16,512]{2,1,0:T(8,128)}, u32[]{:S(2)}, u32[]{:S(2)}) collective-permute-start(f32[128,16,512]{2,1,0:T(8,128)} %param.8), channel_id=1, source_target_pairs={{4,0},{8,4},{12,8},{16,12},{20,16},{24,20},{28,24},{32,28},{36,32}... | collective-permute-start | bytes 12582920 | tf_op jit(solution)/shard_map/ppermute | solution.py:19
  175.6 5.6 %copy-start.1 = (f32[512,512]{1,0:T(8,128)S(1)}, f32[512,512]{1,0:T(8,128)}, u32[]{:S(2)}) copy-start(f32[512,512]{1,0:T(8,128)} %param.12) | copy-start | bytes 3145732
where the time goes:
time: 262 us; the launch traced here: 257 us
  blocking collectives  104 us (40%)
  waiting for transfers between devices  87.5 us (33%)
  matrix products  28.4 us (11%)
  local copies, waits for them, and re-layouts  27.5 us (10%)
  starting transfers between devices  7.4 us (3%)
    ppermute x1, waiting for transfers between devices, with_halo(): before = lax.ppermute(last, axis, up)  81.7 us
    all_to_all x1, blocking collectives, per_device(): lax.all_to_all(smoothed, 'sky', split_axis=1, concat_axis=0, tiled=True)  52.3 us
    all_to_all x1, blocking collectives, per_device(): return lax.all_to_all(mixed, 'sky', split_axis=0, concat_axis=1, tiled=True)  51.9 us
    all_to_all x2, local copies, waits for them, and re-layouts, per_device(): lax.all_to_all(smoothed, 'sky', split_axis=1, concat_axis=0, tiled=True)  10.8 us
    dot_general x1, matrix products, per_device(): jnp.einsum('gh,hcv->gcv', beam_rows, lax.all_to_all(smoothed, 'sky', spli...  9.88 us
    dot_general x1, matrix products, per_device(): jnp.einsum('hcw,vw->hcv', interp, beam_cols, precision=lax.Precision.HIGH...  9.29 us
    dot_general x1, matrix products, per_device(): jnp.einsum('ce,hew->hcw', band, extended, precision=lax.Precision.HIGHEST)  9.21 us
    all_to_all x2, local copies, waits for them, and re-layouts, per_device(): return lax.all_to_all(mixed, 'sky', split_axis=0, concat_axis=1, tiled=True)  8.52 us
  transfers between devices with their start and end apart: 2, of which 2 were waited for; matrix products, arithmetic and copies ran while one was open for 2% of the time, Pallas kernels for 0%

commit v1 on v0

v1 whole, which is shorter than its diff:
```python
import functools

import jax
import jax.numpy as jnp
from jax import lax
from jax.experimental import pallas as pl
from jax.experimental.pallas import tpu as pltpu
from jax.sharding import PartitionSpec as P

BLK = 4
S_MAX = 12
RADIUS = 4
BAND = 8
MESH = pl.DeviceIdType.MESH
BF16 = jnp.bfloat16
F32 = jnp.float32


def split(x):
    high = x.astype(BF16)
    return high, (x - high.astype(F32)).astype(BF16)


def dot(a, b):
    return jnp.dot(a, b, preferred_element_type=F32)


def iota(shape, dim):
    return lax.broadcasted_iota(jnp.int32, shape, dim)


def kernel(
    groups, skies, cube, shifts, halfwidth, taps, beam_rows, beam_cols, out,
    own, left_in, right_in, spread, spread_low, edge_out, edge_in, cols, cols_pair, rows, row_ops, chan_op,
    local_sem, send_sem, recv_sem, edge_send, edge_recv,
):
    chunks, size, width = cube.shape
    chans = size // BAND
    reach = S_MAX + RADIUS
    group, sky = lax.axis_index("chan"), lax.axis_index("sky")
    right, left = lax.rem(group + 1, groups), lax.rem(group + groups - 1, groups)
    has_up, has_down = sky > 0, sky < skies - 1

    barrier = pltpu.get_barrier_semaphore()
    pl.semaphore_signal(barrier, inc=1, device_id={"chan": left}, device_id_type=MESH)
    pl.semaphore_signal(barrier, inc=1, device_id={"chan": right}, device_id_type=MESH)

    @pl.when(has_up)
    def _():
        pl.semaphore_signal(barrier, inc=1, device_id={"sky": sky - 1}, device_id_type=MESH)

    @pl.when(has_down)
    def _():
        pl.semaphore_signal(barrier, inc=1, device_id={"sky": sky + 1}, device_id_type=MESH)

    pl.semaphore_wait(barrier, 2 + has_up.astype(jnp.int32) + has_down.astype(jnp.int32))

    def to_right(at):
        return pltpu.make_async_remote_copy(
            src_ref=cube.at[at], dst_ref=left_in.at[at], send_sem=send_sem.at[0, at], recv_sem=recv_sem.at[0, at],
            device_id={"chan": right}, device_id_type=MESH)

    def to_left(at):
        return pltpu.make_async_remote_copy(
            src_ref=cube.at[at], dst_ref=right_in.at[at], send_sem=send_sem.at[1, at], recv_sem=recv_sem.at[1, at],
            device_id={"chan": left}, device_id_type=MESH)

    @pl.loop(0, chunks // 2)
    def _(step):
        for at in (step, chunks - 1 - step):
            to_right(at).start()
            to_left(at).start()

    height = chunks * BAND
    local = [
        pltpu.make_async_copy(cube, own, local_sem.at[0]),
        pltpu.make_async_copy(beam_cols, cols, local_sem.at[1]),
    ]
    for part in range(3):
        block = lax.rem(sky + skies + part - 1, skies)
        local.append(pltpu.make_async_copy(
            beam_rows.at[pl.ds(pl.multiple_of(sky * height, height), height),
                         pl.ds(pl.multiple_of(block * height, height), height)],
            rows.at[:, pl.ds(part * height, height)], local_sem.at[2 + part]))
    for copy in local:
        copy.start()

    chan = iota((chans, 128), 0)
    place = iota((chans, 128), 1)
    offsets = jnp.zeros((chans, 128), jnp.int32)
    limits = jnp.zeros((chans, 2 * RADIUS + 1), jnp.int32)
    for block in range(chans // BLK):
        offsets = jnp.where(chan // BLK == block, shifts[block], offsets)
        limits = jnp.where(iota(limits.shape, 0) // BLK == block, halfwidth[block], limits)
    masked = jnp.where(jnp.abs(iota(limits.shape, 1) - RADIUS) <= limits, taps[...], 0.0)
    weights = masked / jnp.sum(masked, axis=1, keepdims=True)
    band = jnp.zeros((chans, 128), F32)
    for tap in range(2 * RADIUS + 1):
        band = band + jnp.where(place == chan + reach + offsets + (tap - RADIUS), weights[:, tap:tap + 1], 0.0)
    first = jnp.where(group == 0, chans, 0)
    last = jnp.where(group == groups - 1, 2 * chans, 3 * chans)
    band = jnp.where((place >= first) & (place < last), band, 0.0)
    column = iota((128, 3 * size), 1)
    pick = (iota((128, 3 * size), 0) == column // size * chans + column % chans).astype(BF16)
    same_row = iota((size, 3 * size), 0) // chans == iota((size, 3 * size), 1) % size // chans
    for at, part in enumerate(split(band)):
        wide = jnp.concatenate([dot(part, pick)] * BAND, axis=0)
        chan_op[pl.ds(at * size, size), :] = jnp.where(same_row, wide, 0.0).astype(BF16)

    for copy in local:
        copy.wait()
    high, low = split(cols[...])
    cols_pair[0] = high
    cols_pair[1] = low

    pick = (iota((128, 3 * size), 0) == column // chans).astype(BF16)
    same_chan = iota((size, 3 * size), 0) % chans == iota((size, 3 * size), 1) % chans
    for at in range(chunks):
        start = height + (at - 1) * BAND
        near = rows[pl.ds(at * BAND, BAND), start:start + 3 * BAND]
        near = jnp.concatenate([near, jnp.zeros((BAND, 128 - 3 * BAND), F32)], axis=1)
        high, low = split(near)
        for half, part in enumerate((high, low)):
            wide = dot(part, pick)
            wide = jnp.broadcast_to(wide[:, None, :], (BAND, chans, 3 * size)).reshape(size, 3 * size)
            row_ops[at, pl.ds(half * size, size), :] = jnp.where(same_chan, wide, 0.0).astype(BF16)

    def keep(at, value):
        high, low = split(value)
        spread[at] = high
        spread_low[at] = low

    def smooth(at):
        to_right(at).wait_recv()
        to_left(at).wait_recv()
        total = jnp.zeros((size, width), F32)
        for part, ref in enumerate((left_in, own, right_in)):
            high, low = split(ref[at])
            op = chan_op[:, part * size:(part + 1) * size]
            both = dot(op, high)
            total = total + (both[:size] + both[size:] + dot(op[:size], low))
        high, low = split(total)
        across = (((1,), (1,)), ((), ()))
        both = lax.dot_general(jnp.concatenate([high, low], axis=0), cols_pair[0], across, preferred_element_type=F32)
        return both[:size] + both[size:] + lax.dot_general(high, cols_pair[1], across, preferred_element_type=F32)

    def finish(at):
        op = row_ops[at]
        both = dot(op, spread[pl.ds(at, 3)].reshape(3 * size, width))
        out[at] = both[:size] + both[size:] + dot(op[:size], spread_low[pl.ds(at, 3)].reshape(3 * size, width))

    for side, at in enumerate((0, chunks - 1)):
        value = smooth(at)
        edge_out[side] = value
        keep(at + 1, value)

    @pl.loop(1, 2)
    def _(step):
        for at in (step, chunks - 1 - step):
            keep(at + 1, smooth(at))

    up = pltpu.make_async_remote_copy(
        src_ref=edge_out.at[0], dst_ref=edge_in.at[1], send_sem=edge_send.at[0], recv_sem=edge_recv.at[1],
        device_id={"sky": sky - 1}, device_id_type=MESH)
    down = pltpu.make_async_remote_copy(
        src_ref=edge_out.at[1], dst_ref=edge_in.at[0], send_sem=edge_send.at[1], recv_sem=edge_recv.at[0],
        device_id={"sky": sky + 1}, device_id_type=MESH)

    @pl.when(has_up)
    def _():
        up.start()

    @pl.when(has_down)
    def _():
        down.start()

    @pl.loop(2, chunks // 2)
    def _(step):
        for at in (step, chunks - 1 - step):
            keep(at + 1, smooth(at))
        finish(step - 1)
        finish(chunks - step)

    for at in (chunks // 2 - 1, chunks // 2):
        finish(at)

    @pl.when(has_up)
    def _():
        down.wait_recv()
        keep(0, edge_in[0])
        up.wait_send()

    @pl.when(has_down)
    def _():
        up.wait_recv()
        keep(chunks + 1, edge_in[1])
        down.wait_send()

    @pl.when(jnp.logical_not(has_up))
    def _():
        keep(0, jnp.zeros((size, width), F32))

    @pl.when(jnp.logical_not(has_down))
    def _():
        keep(chunks + 1, jnp.zeros((size, width), F32))

    finish(0)
    finish(chunks - 1)

    @pl.loop(0, chunks)
    def _(at):
        to_right(at).wait_send()
        to_left(at).wait_send()


def solution(mesh):
    groups, skies = mesh.shape["chan"], mesh.shape["sky"]

    def per_device(cube, shifts, halfwidth, taps, beam_rows, beam_cols):
        height, chans, width = cube.shape
        chunks, size = height // BAND, BAND * chans
        anywhere = pl.BlockSpec(memory_space=pl.ANY)
        vmem = pl.BlockSpec(memory_space=pltpu.VMEM)
        smem = pl.BlockSpec(memory_space=pltpu.SMEM)
        whole = (chunks, size, width)
        result = pl.pallas_call(
            functools.partial(kernel, groups, skies),
            out_shape=jax.ShapeDtypeStruct(whole, F32),
            in_specs=[anywhere, smem, smem, vmem, anywhere, anywhere],
            out_specs=vmem,
            scratch_shapes=[
                pltpu.VMEM(whole, F32),
                pltpu.VMEM(whole, F32),
                pltpu.VMEM(whole, F32),
                pltpu.VMEM((chunks + 2, size, width), BF16),
                pltpu.VMEM((chunks + 2, size, width), BF16),
                pltpu.VMEM((2, size, width), F32),
                pltpu.VMEM((2, size, width), F32),
                pltpu.VMEM((width, width), F32),
                pltpu.VMEM((2, width, width), BF16),
                pltpu.VMEM((height, 3 * height), F32),
                pltpu.VMEM((chunks, 2 * size, 3 * size), BF16),
                pltpu.VMEM((2 * size, 3 * size), BF16),
                pltpu.SemaphoreType.DMA((5,)),
                pltpu.SemaphoreType.DMA((2, chunks)),
                pltpu.SemaphoreType.DMA((2, chunks)),
                pltpu.SemaphoreType.DMA((2,)),
                pltpu.SemaphoreType.DMA((2,)),
            ],
            compiler_params=pltpu.CompilerParams(collective_id=0, has_side_effects=True, vmem_limit_bytes=48 << 20),
            name="regrid",
        )(cube.reshape(whole), shifts, halfwidth, taps, beam_rows, beam_cols)
        return result.reshape(cube.shape)

    return jax.shard_map(
        per_device,
        mesh=mesh,
        in_specs=(P("sky", "chan", None), P("chan"), P("chan"), P("chan", None), P(), P()),
        out_specs=P("sky", "chan", None),
        check_vma=False,
    )
```

time: 262 us -> 120 us (0.46); the launches traced: 257 us -> 119 us
  Pallas kernels: 0 us -> 110 us
  blocking collectives: 104 us -> 0 us
  waiting for transfers between devices: 87.5 us -> 0 us
  matrix products: 28.4 us -> 0 us
  local copies, waits for them, and re-layouts: 27.5 us -> 9.5 us
  starting transfers between devices: 7.4 us -> 0 us
    pallas_call x0 -> x1, Pallas kernels: none -> 110 us  [per_device(): pl.pallas_call(functools.partial(kernel, groups, skies), out_shape=jax.Sh...]
    all_to_all x2 -> x0, blocking collectives: 104 us -> none  [the longest x1 52.3 us: per_device(): lax.all_to_all(smoothed, 'sky', split_axis=1, concat_axis=0, tiled=True)]
    ppermute x2 -> x0, waiting for transfers between devices: 87.5 us -> none  [the longest x1 81.7 us: with_halo(): before = lax.ppermute(last, axis, up)]
    dot_general x3 -> x0, matrix products: 28.4 us -> none  [the longest x1 9.88 us: per_device(): jnp.einsum('gh,hcv->gcv', beam_rows, lax.all_to_all(smoothed, 'sky', spli...]
    all_to_all x4 -> x0, local copies, waits for them, and re-layouts: 19.3 us -> none  [the longest x2 10.8 us: per_device(): lax.all_to_all(smoothed, 'sky', split_axis=1, concat_axis=0, tiled=True)]
    unnamed x4 -> x11, local copies, waits for them, and re-layouts: 0.01 us -> 9.5 us
    ppermute x2 -> x0, starting transfers between devices: 7.4 us -> none  [the longest x1 6.12 us: with_halo(): before = lax.ppermute(last, axis, up)]
    dot_general x1 -> x0, local copies, waits for them, and re-layouts: 5.44 us -> none  [per_device(): jnp.einsum('gh,hcv->gcv', beam_rows, lax.all_to_all(smoothed, 'sky', spli...]
  transfers between devices with their start and end apart: 2 -> 0, of which waited for: 2 -> 0; matrix products, arithmetic and copies ran while one was open for 2% -> 0% of each run, Pallas kernels for 0% -> 0%
where the time goes in v1:
time: 120 us; the launch traced here: 119 us
  Pallas kernels  110 us (92%)
  local copies, waits for them, and re-layouts  9.5 us (8%)
    pallas_call x1, Pallas kernels, per_device(): pl.pallas_call(functools.partial(kernel, groups, skies), out_shape=jax.Sh...  110 us
    unnamed x11, local copies, waits for them, and re-layouts  9.5 us

profile of v1, /device:TPU:1, one launch (start us, length us, event | category | flops | bytes accessed | tf_op | source)
XLA Modules:
  0.0 119.4 jit_solution(2770246227029471423)
XLA Ops:
  0.0 0.0 copy-start
  0.0 1.2 %copy-done = f32[512,512]{1,0:T(8,128)S(1)} copy-done((f32[512,512]{1,0:T(8,128)S(1)}, f32[512,512]{1,0:T(8,128)}, u32[]{:S(2)}) %copy-start) | copy-done | bytes 1048600
  1.2 0.0 copy-start.1
  1.2 1.2 %copy-done.1 = f32[512,512]{1,0:T(8,128)S(1)} copy-done((f32[512,512]{1,0:T(8,128)S(1)}, f32[512,512]{1,0:T(8,128)}, u32[]{:S(2)}) %copy-start.1) | copy-done | bytes 1048600
  2.5 0.0 copy-start.2
  2.5 0.7 copy-done.2
  3.1 0.0 copy-start.3
  3.2 0.7 copy-done.3
  3.8 0.0 copy-start.4
  3.8 0.7 copy-done.4
  4.5 109.9 %regrid.1 = f32[16,128,512]{2,1,0:T(8,128)} custom-call(f32[16,128,512]{2,1,0:T(8,128)} %bitcast.3, s32[4]{0:T(128)S(1)} %copy-done.3, s32[4]{0:T(128)S(1)} %copy-done.4, f32[16,9]{1,0:T(8,128)S(1)} %copy-done.2, f32[512,512]{1,0:T(8,128)S(1)} %copy-done, f32[512,512]{1,0:T(8,128)S(1)} %copy-done.1), custom_call_target="tpu_custom_call" | custom-call | tf_op jit(solution)/shard_map/regrid/pallas_call | solution.py:226
  114.4 5.0 %copy.8 = f32[128,16,512]{2,1,0:T(8,128)} copy(f32[128,16,512]{2,1,0:T(8,128)} %bitcast.2) | data formatting | bytes 8388608
Async XLA Ops:
  0.0 1.2 %copy-start = (f32[512,512]{1,0:T(8,128)S(1)}, f32[512,512]{1,0:T(8,128)}, u32[]{:S(2)}) copy-start(f32[512,512]{1,0:T(8,128)} %beam_rows.1) | copy-start | bytes 3145732
  1.2 1.2 %copy-start.1 = (f32[512,512]{1,0:T(8,128)S(1)}, f32[512,512]{1,0:T(8,128)}, u32[]{:S(2)}) copy-start(f32[512,512]{1,0:T(8,128)} %beam_cols.1) | copy-start | bytes 3145732
  2.5 0.7 copy-start.2
  3.1 0.7 copy-start.3
  3.8 0.7 copy-start.4

commit v2 on v1

v2 whole, which is shorter than its diff:
```python
import functools

import jax
import jax.numpy as jnp
from jax import lax
from jax.experimental import pallas as pl
from jax.experimental.pallas import tpu as pltpu
from jax.sharding import PartitionSpec as P

BLK = 4
S_MAX = 12
RADIUS = 4
BAND = 8
MESH = pl.DeviceIdType.MESH
BF16 = jnp.bfloat16
F32 = jnp.float32


def split(x):
    high = x.astype(BF16)
    return high, (x - high.astype(F32)).astype(BF16)


def dot(a, b):
    return jnp.dot(a, b, preferred_element_type=F32)


def iota(shape, dim):
    return lax.broadcasted_iota(jnp.int32, shape, dim)


def kernel(
    groups, skies, cube, shifts_in, halfwidth_in, taps_in, beam_rows, beam_cols, out,
    shifts, halfwidth, taps, own, left_in, right_in, spread, spread_low, tail_op, edge_out, edge_in, cols, cols_pair, rows, row_ops, chan_op,
    local_sem, send_sem, recv_sem, edge_send, edge_recv,
):
    chunks, size, width = cube.shape
    chans = size // BAND
    reach = S_MAX + RADIUS
    group, sky = lax.axis_index("chan"), lax.axis_index("sky")
    has_left, has_right = group > 0, group < groups - 1
    has_up, has_down = sky > 0, sky < skies - 1
    sides = ((has_left, {"chan": group - 1}), (has_right, {"chan": group + 1}),
             (has_up, {"sky": sky - 1}), (has_down, {"sky": sky + 1}))

    barrier = pltpu.get_barrier_semaphore()
    waits = 0
    for there, device in sides:
        @pl.when(there)
        def _():
            pl.semaphore_signal(barrier, inc=1, device_id=device, device_id_type=MESH)

        waits = waits + there.astype(jnp.int32)
    pl.semaphore_wait(barrier, waits)

    def to_right(at):
        return pltpu.make_async_remote_copy(
            src_ref=cube.at[at], dst_ref=left_in.at[at], send_sem=send_sem.at[0, at], recv_sem=recv_sem.at[0, at],
            device_id={"chan": group + 1}, device_id_type=MESH)

    def to_left(at):
        return pltpu.make_async_remote_copy(
            src_ref=cube.at[at], dst_ref=right_in.at[at], send_sem=send_sem.at[1, at], recv_sem=recv_sem.at[1, at],
            device_id={"chan": group - 1}, device_id_type=MESH)

    @pl.loop(0, chunks // 2)
    def _(step):
        for at in (step, chunks - 1 - step):
            @pl.when(has_right)
            def _():
                to_right(at).start()

            @pl.when(has_left)
            def _():
                to_left(at).start()

    height = chunks * BAND
    local = [
        pltpu.make_async_copy(cube, own, local_sem.at[0]),
        pltpu.make_async_copy(beam_cols, cols, local_sem.at[1]),
        pltpu.make_async_copy(shifts_in, shifts, local_sem.at[5]),
        pltpu.make_async_copy(halfwidth_in, halfwidth, local_sem.at[6]),
        pltpu.make_async_copy(taps_in, taps, local_sem.at[7]),
    ]
    for part in range(3):
        block = lax.rem(sky + skies + part - 1, skies)
        local.append(pltpu.make_async_copy(
            beam_rows.at[pl.ds(pl.multiple_of(sky * height, height), height),
                         pl.ds(pl.multiple_of(block * height, height), height)],
            rows.at[:, pl.ds(part * height, height)], local_sem.at[2 + part]))
    for copy in local:
        copy.start()

    @pl.when(jnp.logical_not(has_left))
    def _():
        left_in[...] = jnp.zeros(left_in.shape, F32)

    @pl.when(jnp.logical_not(has_right))
    def _():
        right_in[...] = jnp.zeros(right_in.shape, F32)

    for copy in local:
        copy.wait()

    chan = iota((chans, 128), 0)
    place = iota((chans, 128), 1)
    offsets = jnp.zeros((chans, 128), jnp.int32)
    limits = jnp.zeros((chans, 2 * RADIUS + 1), jnp.int32)
    for block in range(chans // BLK):
        offsets = jnp.where(chan // BLK == block, shifts[block], offsets)
        limits = jnp.where(iota(limits.shape, 0) // BLK == block, halfwidth[block], limits)
    masked = jnp.where(jnp.abs(iota(limits.shape, 1) - RADIUS) <= limits, taps[...], 0.0)
    weights = masked / jnp.sum(masked, axis=1, keepdims=True)
    band = jnp.zeros((chans, 128), F32)
    for tap in range(2 * RADIUS + 1):
        band = band + jnp.where(place == chan + reach + offsets + (tap - RADIUS), weights[:, tap:tap + 1], 0.0)
    column = iota((128, 3 * size), 1)
    pick = (iota((128, 3 * size), 0) == column // size * chans + column % chans).astype(BF16)
    same_row = iota((size, 3 * size), 0) // chans == iota((size, 3 * size), 1) % size // chans
    for at, part in enumerate(split(band)):
        wide = jnp.concatenate([dot(part, pick)] * BAND, axis=0)
        chan_op[pl.ds(at * size, size), :] = jnp.where(same_row, wide, 0.0).astype(BF16)

    high, low = split(cols[...])
    cols_pair[0] = high
    cols_pair[1] = low

    pick = (iota((128, 3 * size), 0) == column // chans).astype(BF16)
    same_chan = iota((size, 3 * size), 0) % chans == iota((size, 3 * size), 1) % chans
    for at in range(chunks):
        start = height + (at - 1) * BAND
        near = rows[pl.ds(at * BAND, BAND), start:start + 3 * BAND]
        near = jnp.concatenate([near, jnp.zeros((BAND, 128 - 3 * BAND), F32)], axis=1)
        high, low = split(near)
        for half, part in enumerate((high, low)):
            wide = dot(part, pick)
            wide = jnp.broadcast_to(wide[:, None, :], (BAND, chans, 3 * size)).reshape(size, 3 * size)
            row_ops[at, pl.ds(half * size, size), :] = jnp.where(same_chan, wide, 0.0).astype(BF16)

    def keep(at, value):
        high, low = split(value)
        spread[at] = high
        spread_low[at] = low

    def arrive(at):
        @pl.when(has_left)
        def _():
            to_right(at).wait_recv()

        @pl.when(has_right)
        def _():
            to_left(at).wait_recv()

    def blend(part, ref, at):
        high, low = split(ref[at])
        op = chan_op[:, part * size:(part + 1) * size]
        both = dot(op, high)
        return both[:size] + both[size:] + dot(op[:size], low)

    def across(total):
        high, low = split(total)
        dims = (((1,), (1,)), ((), ()))
        both = lax.dot_general(jnp.concatenate([high, low], axis=0), cols_pair[0], dims, preferred_element_type=F32)
        return both[:size] + both[size:] + lax.dot_general(high, cols_pair[1], dims, preferred_element_type=F32)

    def smooth(at):
        arrive(at)
        return across(blend(1, own, at) + blend(0, left_in, at) + blend(2, right_in, at))

    def finish(at):
        op = row_ops[at]
        both = dot(op, spread[pl.ds(at, 3)].reshape(3 * size, width))
        out[at] = both[:size] + both[size:] + dot(op[:size], spread_low[pl.ds(at, 3)].reshape(3 * size, width))

    for side, at in enumerate((0, chunks - 1)):
        value = smooth(at)
        edge_out[side] = value
        keep(at + 1, value)

    for at in (1, chunks - 2):
        keep(at + 1, smooth(at))

    up = pltpu.make_async_remote_copy(
        src_ref=edge_out.at[0], dst_ref=edge_in.at[1], send_sem=edge_send.at[0], recv_sem=edge_recv.at[1],
        device_id={"sky": sky - 1}, device_id_type=MESH)
    down = pltpu.make_async_remote_copy(
        src_ref=edge_out.at[1], dst_ref=edge_in.at[0], send_sem=edge_send.at[1], recv_sem=edge_recv.at[0],
        device_id={"sky": sky + 1}, device_id_type=MESH)

    @pl.when(has_up)
    def _():
        up.start()

    @pl.when(has_down)
    def _():
        down.start()

    last = chunks // 2
    keep(last + 1, jnp.zeros((size, width), F32))
    for place in range(3):
        for half in range(2):
            tail_op[pl.ds((3 * half + place) * size, size), :] = row_ops[
                last - 1 + place, pl.ds(half * size, size), (2 - place) * size:(3 - place) * size]

    @pl.loop(2, last - 1)
    def _(step):
        for at in (step, chunks - 1 - step):
            keep(at + 1, smooth(at))
        finish(step - 1)
        finish(chunks - step)

    @pl.when(has_up)
    def _():
        down.wait_recv()
        keep(0, edge_in[0])

    @pl.when(has_down)
    def _():
        up.wait_recv()
        keep(chunks + 1, edge_in[1])

    @pl.when(jnp.logical_not(has_up))
    def _():
        keep(0, jnp.zeros((size, width), F32))

    @pl.when(jnp.logical_not(has_down))
    def _():
        keep(chunks + 1, jnp.zeros((size, width), F32))

    finish(0)
    finish(chunks - 1)
    keep(last, smooth(last - 1))
    ready = blend(1, own, last)
    for at in (last - 2, last + 1, last - 1, last):
        finish(at)

    arrive(last)
    high, low = split(across(ready + blend(0, left_in, last) + blend(2, right_in, last)))
    three = 3 * size
    both = dot(tail_op[...], high)
    share = both[:three] + both[three:] + dot(tail_op[:three, :], low)
    for place in range(3):
        out[last - 1 + place] += share[place * size:(place + 1) * size]

    @pl.when(has_up)
    def _():
        up.wait_send()

    @pl.when(has_down)
    def _():
        down.wait_send()

    @pl.loop(0, chunks)
    def _(at):
        @pl.when(has_right)
        def _():
            to_right(at).wait_send()

        @pl.when(has_left)
        def _():
            to_left(at).wait_send()


def solution(mesh):
    groups, skies = mesh.shape["chan"], mesh.shape["sky"]

    def per_device(cube, shifts, halfwidth, taps, beam_rows, beam_cols):
        height, chans, width = cube.shape
        chunks, size = height // BAND, BAND * chans
        stay = pl.BlockSpec(memory_space=pltpu.HBM)
        whole = (chunks, size, width)
        result = pl.pallas_call(
            functools.partial(kernel, groups, skies),
            out_shape=pltpu.VMEM(whole, F32),
            in_specs=[stay] * 6,
            out_specs=pl.BlockSpec(memory_space=pltpu.VMEM),
            scratch_shapes=[
                pltpu.SMEM(shifts.shape, jnp.int32),
                pltpu.SMEM(halfwidth.shape, jnp.int32),
                pltpu.VMEM(taps.shape, F32),
                pltpu.VMEM(whole, F32),
                pltpu.VMEM(whole, F32),
                pltpu.VMEM(whole, F32),
                pltpu.VMEM((chunks + 2, size, width), BF16),
                pltpu.VMEM((chunks + 2, size, width), BF16),
                pltpu.VMEM((6 * size, size), BF16),
                pltpu.VMEM((2, size, width), F32),
                pltpu.VMEM((2, size, width), F32),
                pltpu.VMEM((width, width), F32),
                pltpu.VMEM((2, width, width), BF16),
                pltpu.VMEM((height, 3 * height), F32),
                pltpu.VMEM((chunks, 2 * size, 3 * size), BF16),
                pltpu.VMEM((2 * size, 3 * size), BF16),
                pltpu.SemaphoreType.DMA((8,)),
                pltpu.SemaphoreType.DMA((2, chunks)),
                pltpu.SemaphoreType.DMA((2, chunks)),
                pltpu.SemaphoreType.DMA((2,)),
                pltpu.SemaphoreType.DMA((2,)),
            ],
            compiler_params=pltpu.CompilerParams(collective_id=0, has_side_effects=True, vmem_limit_bytes=48 << 20),
            name="regrid",
        )(*(pltpu.with_memory_space_constraint(x, pltpu.HBM) for x in (
            cube.reshape(whole), shifts, halfwidth, taps, beam_rows, beam_cols)))
        return result.reshape(cube.shape)

    return jax.shard_map(
        per_device,
        mesh=mesh,
        in_specs=(P("sky", "chan", None), P("chan"), P("chan"), P("chan", None), P(), P()),
        out_specs=P("sky", "chan", None),
        check_vma=False,
    )
```

time: 120 us -> 108 us (0.900)
  local copies, waits for them, and re-layouts: 9.5 us -> 2.02 us
  Pallas kernels: 110 us -> 105 us
    unnamed x11 -> x1, local copies, waits for them, and re-layouts: 9.5 us -> 2.02 us
    pallas_call x1, Pallas kernels: 110 us -> 105 us  [per_device(): pl.pallas_call(functools.partial(kernel, groups, skies), out_shape=pltpu....]
where the time goes in v2:
time: 108 us; the launch traced here: 107 us
  Pallas kernels  105 us (97%)
  local copies, waits for them, and re-layouts  2.02 us (2%)
    pallas_call x1, Pallas kernels, per_device(): pl.pallas_call(functools.partial(kernel, groups, skies), out_shape=pltpu....  105 us

profile of v2, /device:TPU:1, one launch (start us, length us, event | category | flops | bytes accessed | tf_op | source)
XLA Modules:
  0.0 107.3 jit_solution(7648588961135293372)
XLA Ops:
  0.0 105.3 %regrid.1 = f32[16,128,512]{2,1,0:T(8,128)S(1)} custom-call(f32[16,128,512]{2,1,0:T(8,128)} %bitcast.3, s32[4]{0:T(128)} %shifts_in.1, s32[4]{0:T(128)} %halfwidth_in.1, f32[16,9]{1,0:T(8,128)} %taps_in.1, f32[512,512]{1,0:T(8,128)} %beam_rows.1, f32[512,512]{1,0:T(8,128)} %beam_cols.1), custom_call_target="tpu_custom_call" | custom-call | tf_op jit(solution)/shard_map/regrid/pallas_call | solution.py:272
  105.3 2.0 %copy.8 = f32[128,16,512]{2,1,0:T(8,128)} copy(f32[128,16,512]{2,1,0:T(8,128)S(1)} %bitcast.2) | data formatting | bytes 8388608

commit v3 on v2

--- a/solution.py
+++ b/solution.py
@@ -11,6 +11,8 @@
 S_MAX = 12
 RADIUS = 4
 BAND = 8
+AHEAD = 2
+RUN = 4
 MESH = pl.DeviceIdType.MESH
 BF16 = jnp.bfloat16
 F32 = jnp.float32
@@ -31,7 +33,7 @@
 
 def kernel(
     groups, skies, cube, shifts_in, halfwidth_in, taps_in, beam_rows, beam_cols, out,
-    shifts, halfwidth, taps, own, left_in, right_in, spread, spread_low, tail_op, edge_out, edge_in, cols, cols_pair, rows, row_ops, chan_op,
+    shifts, halfwidth, taps, own, left_in, right_in, spread, spread_low, tail_op, edge_out, edge_in, detour, cols, cols_pair, rows, row_ops, chan_op,
     local_sem, send_sem, recv_sem, edge_send, edge_recv,
 ):
     chunks, size, width = cube.shape
@@ -40,6 +42,13 @@
     group, sky = lax.axis_index("chan"), lax.axis_index("sky")
     has_left, has_right = group > 0, group < groups - 1
     has_up, has_down = sky > 0, sky < skies - 1
+    spot = lax.rem(group, RUN)
+    crosses = jnp.where(lax.rem(sky, 2) == 1, has_down, has_up)
+    beyond = jnp.where(lax.rem(sky, 2) == 1, sky + 1, sky - 1)
+    beside = jnp.where(spot == 0, group + 1, group - 1)
+    detours = crosses & ((spot == 0) | (spot == RUN - 1)) & (beside < groups)
+    served = jnp.where(spot == 1, group - 1, group + 1)
+    relays = crosses & ((spot == 1) | (spot == RUN - 2)) & (served < groups)
     sides = ((has_left, {"chan": group - 1}), (has_right, {"chan": group + 1}),
              (has_up, {"sky": sky - 1}), (has_down, {"sky": sky + 1}))
 
@@ -51,7 +60,11 @@
             pl.semaphore_signal(barrier, inc=1, device_id=device, device_id_type=MESH)
 
         waits = waits + there.astype(jnp.int32)
-    pl.semaphore_wait(barrier, waits)
+    @pl.when(detours)
+    def _():
+        pl.semaphore_signal(barrier, inc=1, device_id={"chan": beside, "sky": beyond}, device_id_type=MESH)
+
+    pl.semaphore_wait(barrier, waits + relays.astype(jnp.int32))
 
     def to_right(at):
         return pltpu.make_async_remote_copy(
@@ -63,8 +76,7 @@
             src_ref=cube.at[at], dst_ref=right_in.at[at], send_sem=send_sem.at[1, at], recv_sem=recv_sem.at[1, at],
             device_id={"chan": group - 1}, device_id_type=MESH)
 
-    @pl.loop(0, chunks // 2)
-    def _(step):
+    def send(step):
         for at in (step, chunks - 1 - step):
             @pl.when(has_right)
             def _():
@@ -73,6 +85,9 @@
             @pl.when(has_left)
             def _():
                 to_left(at).start()
+
+    for step in range(AHEAD):
+        send(step)
 
     height = chunks * BAND
     local = [
@@ -177,23 +192,37 @@
         edge_out[side] = value
         keep(at + 1, value)
 
+    def edge(side, device):
+        return pltpu.make_async_remote_copy(
+            src_ref=edge_out.at[side], dst_ref=edge_in.at[1 - side], send_sem=edge_send.at[side],
+            recv_sem=edge_recv.at[1 - side], device_id=device, device_id_type=MESH)
+
+    up, down = edge(0, {"sky": sky - 1}), edge(1, {"sky": sky + 1})
+    odd = lax.rem(sky, 2) == 1
+
+    def first_leg(side):
+        return pltpu.make_async_remote_copy(
+            src_ref=edge_out.at[side], dst_ref=detour, send_sem=edge_send.at[side], recv_sem=edge_recv.at[2],
+            device_id={"chan": beside}, device_id_type=MESH)
+
+    def second_leg(side):
+        return pltpu.make_async_remote_copy(
+            src_ref=detour, dst_ref=edge_in.at[1 - side], send_sem=edge_send.at[2],
+            recv_sem=edge_recv.at[1 - side], device_id={"chan": served, "sky": beyond}, device_id_type=MESH)
+
+    for side, there, copy, turn in ((0, has_up, up, jnp.logical_not(odd)), (1, has_down, down, odd)):
+        @pl.when(there & jnp.logical_not(detours & turn))
+        def _():
+            copy.start()
+
+        @pl.when(detours & turn)
+        def _():
+            first_leg(side).start()
+
+    for step in range(AHEAD, AHEAD + 2):
+        send(step)
     for at in (1, chunks - 2):
         keep(at + 1, smooth(at))
-
-    up = pltpu.make_async_remote_copy(
-        src_ref=edge_out.at[0], dst_ref=edge_in.at[1], send_sem=edge_send.at[0], recv_sem=edge_recv.at[1],
-        device_id={"sky": sky - 1}, device_id_type=MESH)
-    down = pltpu.make_async_remote_copy(
-        src_ref=edge_out.at[1], dst_ref=edge_in.at[0], send_sem=edge_send.at[1], recv_sem=edge_recv.at[0],
-        device_id={"sky": sky + 1}, device_id_type=MESH)
-
-    @pl.when(has_up)
-    def _():
-        up.start()
-
-    @pl.when(has_down)
-    def _():
-        down.start()
 
     last = chunks // 2
     keep(last + 1, jnp.zeros((size, width), F32))
@@ -202,12 +231,29 @@
             tail_op[pl.ds((3 * half + place) * size, size), :] = row_ops[
                 last - 1 + place, pl.ds(half * size, size), (2 - place) * size:(3 - place) * size]
 
-    @pl.loop(2, last - 1)
-    def _(step):
+    def tend(step):
+        @pl.when(step + AHEAD < last)
+        def _():
+            send(step + AHEAD)
+
         for at in (step, chunks - 1 - step):
             keep(at + 1, smooth(at))
         finish(step - 1)
         finish(chunks - step)
+
+    @pl.loop(2, last - 3)
+    def _(step):
+        tend(step)
+
+    for side, turn in ((0, jnp.logical_not(odd)), (1, odd)):
+        @pl.when(relays & turn)
+        def _():
+            first_leg(side).wait_recv()
+            second_leg(side).start()
+
+    @pl.loop(last - 3, last - 1)
+    def _(step):
+        tend(step)
 
     @pl.when(has_up)
     def _():
@@ -241,6 +287,11 @@
     share = both[:three] + both[three:] + dot(tail_op[:three, :], low)
     for place in range(3):
         out[last - 1 + place] += share[place * size:(place + 1) * size]
+
+    for side, turn in ((0, jnp.logical_not(odd)), (1, odd)):
+        @pl.when(relays & turn)
+        def _():
+            second_leg(side).wait_send()
 
     @pl.when(has_up)
     def _():
@@ -286,6 +337,7 @@
                 pltpu.VMEM((6 * size, size), BF16),
                 pltpu.VMEM((2, size, width), F32),
                 pltpu.VMEM((2, size, width), F32),
+                pltpu.VMEM((size, width), F32),
                 pltpu.VMEM((width, width), F32),
                 pltpu.VMEM((2, width, width), BF16),
                 pltpu.VMEM((height, 3 * height), F32),
@@ -294,8 +346,8 @@
                 pltpu.SemaphoreType.DMA((8,)),
                 pltpu.SemaphoreType.DMA((2, chunks)),
                 pltpu.SemaphoreType.DMA((2, chunks)),
-                pltpu.SemaphoreType.DMA((2,)),
-                pltpu.SemaphoreType.DMA((2,)),
+                pltpu.SemaphoreType.DMA((3,)),
+                pltpu.SemaphoreType.DMA((3,)),
             ],
             compiler_params=pltpu.CompilerParams(collective_id=0, has_side_effects=True, vmem_limit_bytes=48 << 20),
             name="regrid",

time: 108 us -> 104 us (0.963)
  the two profiles are of different devices: /device:TPU:1 before, /device:TPU:169 now
where the time goes in v3:
time: 104 us
  Pallas kernels  102 us (98%)
  local copies, waits for them, and re-layouts  2.02 us (2%)
    pallas_call x1, Pallas kernels, per_device(): pl.pallas_call(functools.partial(kernel, groups, skies), out_shape=pltpu....  102 us

profile of v3, /device:TPU:169, one launch (start us, length us, event | category | flops | bytes accessed | tf_op | source)
XLA Modules:
  0.0 103.7 jit_solution(2375800787598442469)
XLA Ops:
  0.0 101.7 %regrid.1 = f32[16,128,512]{2,1,0:T(8,128)S(1)} custom-call(f32[16,128,512]{2,1,0:T(8,128)} %bitcast.3, s32[4]{0:T(128)} %shifts_in.1, s32[4]{0:T(128)} %halfwidth_in.1, f32[16,9]{1,0:T(8,128)} %taps_in.1, f32[512,512]{1,0:T(8,128)} %beam_rows.1, f32[512,512]{1,0:T(8,128)} %beam_cols.1), custom_call_target="tpu_custom_call" | custom-call | tf_op jit(solution)/shard_map/regrid/pallas_call | solution.py:323
  101.7 2.0 %copy.8 = f32[128,16,512]{2,1,0:T(8,128)} copy(f32[128,16,512]{2,1,0:T(8,128)S(1)} %bitcast.2) | data formatting | bytes 8388608

commit v4 on v3

v4 whole, which is shorter than its diff:
```python
import functools

import jax
import jax.numpy as jnp
from jax import lax
from jax.experimental import pallas as pl
from jax.experimental.pallas import tpu as pltpu
from jax.sharding import PartitionSpec as P

BLK = 4
S_MAX = 12
RADIUS = 4
BAND = 8
SLOTS = 12
AHEAD = 2
RUN = 4
INNER = 8
MESH = pl.DeviceIdType.MESH
BF16 = jnp.bfloat16
F32 = jnp.float32
ACROSS = (((1,), (1,)), ((), ()))


def split(x):
    high = x.astype(BF16)
    return high, (x - high.astype(F32)).astype(BF16)


def dot(a, b):
    return jnp.dot(a, b, preferred_element_type=F32)


def dot_across(a, b):
    return lax.dot_general(a, b, ACROSS, preferred_element_type=F32)


def iota(shape, dim):
    return lax.broadcasted_iota(jnp.int32, shape, dim)


def ones_where(condition):
    return jnp.where(condition, 1.0, 0.0).astype(BF16)


def deepen(x):
    return jnp.concatenate([x, jnp.zeros((128 - x.shape[0], x.shape[1]), x.dtype)], axis=0)


def need(band):
    shape = band.shape
    row, lane = iota(shape, 0), iota(shape, 1)
    ones, before = jnp.ones((128, 128), BF16), ones_where(iota((128, 128), 0) < iota((128, 128), 1))
    pattern = ones_where(band != 0.0)
    high, low = split(band)
    touched = ones_where(dot_across(ones[:shape[0]], deepen(pattern)) > 0.5)
    few_out = dot(touched, ones)
    pick = ones_where((dot(touched, before).astype(jnp.int32) == row) & (touched > 0.5))
    send_out = dot(pick, deepen(high)) + dot(pick, deepen(low))
    touched = ones_where(dot(pattern, ones) > 0.5)
    rank = dot(ones_where(lane < row), deepen(touched)).astype(jnp.int32)
    receive_out = jnp.where((rank == lane) & (touched > 0.5), 1.0, 0.0)
    touched = ones_where(dot(ones[:shape[0]], deepen(pattern)) > 0.5)
    few_raw = dot(touched, ones)
    pick = ones_where((dot(touched, before).astype(jnp.int32) == row) & (touched > 0.5))
    outs = few_out <= few_raw
    send = jnp.where(outs, send_out, pick.astype(F32))
    high = jnp.where(outs, receive_out, dot_across(high, deepen(pick)))
    low = jnp.where(outs, 0.0, dot_across(low, deepen(pick)))
    return send, (high.astype(BF16), low.astype(BF16)), jnp.minimum(few_out, few_raw)


def kernel(lean, groups, skies, *refs):
    cube, shifts_in, halfwidth_in, taps_in, beam_rows, beam_cols, out, *refs = refs
    if lean:
        flag, needs, asked, for_left, for_right, send_ops, receive_ops, near_flags, far_flags, my_flag, *refs = refs
        need_send, need_recv, flag_send, flag_recv, *refs = refs
    (shifts, halfwidth, taps, own, left_in, right_in, spread, spread_low, tail_op, edge_out, edge_in, detour, cols,
     cols_pair, rows, row_ops, chan_op, local_sem, send_sem, recv_sem, edge_send, edge_recv) = refs
    chunks, size, width = cube.shape
    chans = size // BAND
    reach = S_MAX + RADIUS
    thin = SLOTS * BAND
    last = chunks // 2
    group, sky = lax.axis_index("chan"), lax.axis_index("sky")
    has_left, has_right = group > 0, group < groups - 1
    has_up, has_down = sky > 0, sky < skies - 1
    inner = min(INNER, groups)
    outer = groups // inner
    at_inner, at_outer = lax.rem(group, inner), group // inner
    spot = lax.rem(group, RUN)
    odd = lax.rem(sky, 2) == 1
    crosses = jnp.where(odd, has_down, has_up)
    beyond = jnp.where(odd, sky + 1, sky - 1)
    beside = jnp.where(spot == 0, group + 1, group - 1)
    detours = crosses & ((spot == 0) | (spot == RUN - 1)) & (beside < groups)
    served = jnp.where(spot == 1, group - 1, group + 1)
    relays = crosses & ((spot == 1) | (spot == RUN - 2)) & (served < groups)

    barrier = pltpu.get_barrier_semaphore()
    sides = [(has_left, {"chan": group - 1}), (has_right, {"chan": group + 1}),
             (has_up, {"sky": sky - 1}), (has_down, {"sky": sky + 1})]
    near = [(at_inner != peer, {"chan": at_outer * inner + peer}) for peer in range(inner)] if lean else []
    far = [(at_outer != peer, {"chan": peer * inner + at_inner}) for peer in range(outer)] if lean else []
    waits = relays.astype(jnp.int32)
    for there, device in sides + near + far:
        @pl.when(there)
        def _():
            pl.semaphore_signal(barrier, inc=1, device_id=device, device_id_type=MESH)

        waits = waits + there.astype(jnp.int32)

    @pl.when(detours)
    def _():
        pl.semaphore_signal(barrier, inc=1, device_id={"chan": beside, "sky": beyond}, device_id_type=MESH)

    height = chunks * BAND
    local = [
        pltpu.make_async_copy(shifts_in, shifts, local_sem.at[5]),
        pltpu.make_async_copy(halfwidth_in, halfwidth, local_sem.at[6]),
        pltpu.make_async_copy(taps_in, taps, local_sem.at[7]),
        pltpu.make_async_copy(cube, own, local_sem.at[0]),
        pltpu.make_async_copy(beam_cols, cols, local_sem.at[1]),
    ]
    for part in range(3):
        block = lax.rem(sky + skies + part - 1, skies)
        local.append(pltpu.make_async_copy(
            beam_rows.at[pl.ds(pl.multiple_of(sky * height, height), height),
                         pl.ds(pl.multiple_of(block * height, height), height)],
            rows.at[:, pl.ds(part * height, height)], local_sem.at[2 + part]))
    for copy in local:
        copy.start()
    for copy in local[:3]:
        copy.wait()

    chan = iota((chans, 128), 0)
    place = iota((chans, 128), 1)
    offsets = jnp.zeros((chans, 128), jnp.int32)
    limits = jnp.zeros((chans, 2 * RADIUS + 1), jnp.int32)
    for block in range(chans // BLK):
        offsets = jnp.where(chan // BLK == block, shifts[block], offsets)
        limits = jnp.where(iota(limits.shape, 0) // BLK == block, halfwidth[block], limits)
    masked = jnp.where(jnp.abs(iota(limits.shape, 1) - RADIUS) <= limits, taps[...], 0.0)
    weights = masked / jnp.sum(masked, axis=1, keepdims=True)

    def slab(base):
        band = jnp.zeros((chans, 128), F32)
        for tap in range(2 * RADIUS + 1):
            spot = chan + reach + offsets + (tap - RADIUS) - base
            band = band + jnp.where((place == spot) & (place < chans), weights[:, tap:tap + 1], 0.0)
        return band

    left_band = jnp.where(has_left, slab(0), 0.0)
    right_band = jnp.where(has_right, slab(2 * chans), 0.0)
    bands = (left_band, slab(chans), right_band)

    if lean:
        receives = []
        over = jnp.zeros((chans, 128), F32)
        for side, band in enumerate((bands[0], bands[2])):
            send, receive, count = need(band)
            needs[side] = send
            receives.append(receive)
            over = over + jnp.where(count > SLOTS + 0.5, 1.0, 0.0)
        my_flag[0] = over[:8]
        near_flags[at_inner] = over[:8]

        @pl.when(jnp.logical_not(has_left))
        def _():
            asked[0] = jnp.zeros((chans, 128), F32)

        @pl.when(jnp.logical_not(has_right))
        def _():
            asked[1] = jnp.zeros((chans, 128), F32)

    pl.semaphore_wait(barrier, waits)

    def thinned(ref, at, raw):
        return ref.at[at] if raw else ref.at[at, pl.ds(0, thin)]

    def to_right(at, raw):
        return pltpu.make_async_remote_copy(
            src_ref=cube.at[at] if raw else for_right.at[at], dst_ref=thinned(left_in, at, raw),
            send_sem=send_sem.at[0, at], recv_sem=recv_sem.at[0, at],
            device_id={"chan": group + 1}, device_id_type=MESH)

    def to_left(at, raw):
        return pltpu.make_async_remote_copy(
            src_ref=cube.at[at] if raw else for_left.at[at], dst_ref=thinned(right_in, at, raw),
            send_sem=send_sem.at[1, at], recv_sem=recv_sem.at[1, at],
            device_id={"chan": group - 1}, device_id_type=MESH)

    def send(step, raw):
        for at in (step, chunks - 1 - step):
            @pl.when(has_right)
            def _():
                to_right(at, raw).start()

            @pl.when(has_left)
            def _():
                to_left(at, raw).start()

    def ask(side):
        return pltpu.make_async_remote_copy(
            src_ref=needs.at[side], dst_ref=asked.at[1 - side], send_sem=need_send.at[side],
            recv_sem=need_recv.at[1 - side], device_id=sides[side][1], device_id_type=MESH)

    def tell(stage, peer):
        target, mine = ((near_flags, at_inner), (far_flags, at_outer))[stage]
        return pltpu.make_async_remote_copy(
            src_ref=my_flag.at[stage], dst_ref=target.at[mine], send_sem=flag_send.at[stage, peer],
            recv_sem=flag_recv.at[stage, mine], device_id=(near, far)[stage][peer][1], device_id_type=MESH)

    def told(stage, peer):
        source = (near_flags, far_flags)[stage].at[peer]
        return pltpu.make_async_remote_copy(
            src_ref=my_flag.at[stage], dst_ref=source, send_sem=flag_send.at[stage, peer],
            recv_sem=flag_recv.at[stage, peer], device_id=(near, far)[stage][peer][1], device_id_type=MESH)

    def each(stage, act):
        for peer, (there, _) in enumerate((near, far)[stage]):
            @pl.when(there)
            def _():
                act(peer)

    if lean:
        for side in range(2):
            @pl.when(sides[side][0])
            def _():
                ask(side).start()

        each(0, lambda peer: tell(0, peer).start())

    send(0, True)
    if not lean:
        send(1, True)

    @pl.when(jnp.logical_not(has_left))
    def _():
        left_in[...] = jnp.zeros(left_in.shape, F32)

    @pl.when(jnp.logical_not(has_right))
    def _():
        right_in[...] = jnp.zeros(right_in.shape, F32)

    for copy in local[3:]:
        copy.wait()

    def apply(op, value, rows_out):
        high, low = split(value)
        both = dot(op, high)
        return both[:rows_out] + both[rows_out:] + dot(op[:rows_out], low)

    def reduce_for(step):
        for at in (step, chunks - 1 - step):
            for side, ref in enumerate((for_left, for_right)):
                ref[at] = apply(send_ops[side], own[at], thin)

    if lean:
        for side in range(2):
            @pl.when(sides[side][0])
            def _():
                ask(1 - side).wait_recv()

        pick = ones_where(iota((128, 128), 0) == iota((128, 128), 1) % chans)
        same_row = iota((128, 128), 0) % BAND == iota((128, 128), 1) // chans
        for side in range(2):
            for half, part in enumerate(split(asked[side])):
                wide = jnp.broadcast_to(dot(part, pick)[:, None, :], (chans, BAND, 128)).reshape(128, 128)
                send_ops[side, pl.ds(half * thin, thin), :] = jnp.where(same_row, wide, 0.0)[:thin].astype(BF16)
        reduce_for(1)

    pick = ones_where(iota((128, size), 0) == iota((128, size), 1) % chans)
    same_row = iota((size, size), 0) // chans == iota((size, size), 1) // chans
    for slot, band in enumerate(bands):
        for half, part in enumerate(split(band)):
            wide = jnp.concatenate([dot(part, pick)] * BAND, axis=0)
            chan_op[pl.ds(half * size, size), pl.ds(slot * size, size)] = jnp.where(same_row, wide, 0.0).astype(BF16)
    if lean:
        send(1, False)
        pick = ones_where(iota((128, 128), 0) == iota((128, 128), 1) // BAND)
        same_row = iota((size, 128), 0) // chans == iota((size, 128), 1) % BAND
        for side, receive in enumerate(receives):
            for half, part in enumerate(receive):
                wide = jnp.concatenate([dot(part, pick)] * BAND, axis=0)
                receive_ops[side, pl.ds(half * size, size), :] = jnp.where(same_row, wide, 0.0).astype(BF16)
        reduce_for(2)

    high, low = split(cols[...])
    cols_pair[0] = high
    cols_pair[1] = low

    pick = ones_where(iota((128, 3 * size), 0) == iota((128, 3 * size), 1) // chans)
    same_chan = iota((size, 3 * size), 0) % chans == iota((size, 3 * size), 1) % chans
    for at in range(chunks):
        start = height + (at - 1) * BAND
        close = rows[pl.ds(at * BAND, BAND), start:start + 3 * BAND]
        close = jnp.concatenate([close, jnp.zeros((BAND, 128 - 3 * BAND), F32)], axis=1)
        for half, part in enumerate(split(close)):
            wide = dot(part, pick)
            wide = jnp.broadcast_to(wide[:, None, :], (BAND, chans, 3 * size)).reshape(size, 3 * size)
            row_ops[at, pl.ds(half * size, size), :] = jnp.where(same_chan, wide, 0.0).astype(BF16)

    def keep(at, value):
        high, low = split(value)
        spread[at] = high
        spread_low[at] = low

    def arrive(at, raw):
        @pl.when(has_left)
        def _():
            to_right(at, raw).wait_recv()

        @pl.when(has_right)
        def _():
            to_left(at, raw).wait_recv()

    def blend(part, ref, at, raw=True):
        if raw:
            return apply(chan_op[:, part * size:(part + 1) * size], ref[at], size)
        return apply(receive_ops[part // 2, :, :thin], ref[at, pl.ds(0, thin)], size)

    def across(total):
        high, low = split(total)
        both = dot_across(jnp.concatenate([high, low], axis=0), cols_pair[0])
        return both[:size] + both[size:] + dot_across(high, cols_pair[1])

    def smooth(at, raw):
        arrive(at, raw)
        return across(blend(1, own, at) + blend(0, left_in, at, raw) + blend(2, right_in, at, raw))

    def finish(at):
        op = row_ops[at]
        both = dot(op, spread[pl.ds(at, 3)].reshape(3 * size, width))
        out[at] = both[:size] + both[size:] + dot(op[:size], spread_low[pl.ds(at, 3)].reshape(3 * size, width))

    whole = not lean
    for side, at in enumerate((0, chunks - 1)):
        value = smooth(at, True)
        edge_out[side] = value
        keep(at + 1, value)
    if lean:
        each(0, lambda peer: told(0, peer).wait_recv())
        total = near_flags[0]
        for peer in range(1, inner):
            total = total + near_flags[peer]
        my_flag[1] = total
        far_flags[at_outer] = total

    def edge(side, device):
        return pltpu.make_async_remote_copy(
            src_ref=edge_out.at[side], dst_ref=edge_in.at[1 - side], send_sem=edge_send.at[side],
            recv_sem=edge_recv.at[1 - side], device_id=device, device_id_type=MESH)

    up, down = edge(0, {"sky": sky - 1}), edge(1, {"sky": sky + 1})

    def first_leg(side):
        return pltpu.make_async_remote_copy(
            src_ref=edge_out.at[side], dst_ref=detour, send_sem=edge_send.at[side], recv_sem=edge_recv.at[2],
            device_id={"chan": beside}, device_id_type=MESH)

    def second_leg(side):
        return pltpu.make_async_remote_copy(
            src_ref=detour, dst_ref=edge_in.at[1 - side], send_sem=edge_send.at[2],
            recv_sem=edge_recv.at[1 - side], device_id={"chan": served, "sky": beyond}, device_id_type=MESH)

    turns = ((0, jnp.logical_not(odd)), (1, odd))
    for side, turn in turns:
        there, copy = ((has_up, up), (has_down, down))[side]

        @pl.when(there & jnp.logical_not(detours & turn))
        def _():
            copy.start()

        @pl.when(detours & turn)
        def _():
            first_leg(side).start()

    for step in range(2, AHEAD + 2):
        send(step, whole)
        if lean:
            reduce_for(step + 1)
    for at in (1, chunks - 2):
        keep(at + 1, smooth(at, whole))
    if lean:
        each(1, lambda peer: tell(1, peer).start())

    keep(last + 1, jnp.zeros((size, width), F32))
    for spot in range(3):
        for half in range(2):
            tail_op[pl.ds((3 * half + spot) * size, size), :] = row_ops[
                last - 1 + spot, pl.ds(half * size, size), (2 - spot) * size:(3 - spot) * size]

    def tend(step):
        @pl.when(step + AHEAD < last)
        def _():
            send(step + AHEAD, whole)

        if lean:
            @pl.when(step + AHEAD + 1 < last)
            def _():
                reduce_for(step + AHEAD + 1)

        for at in (step, chunks - 1 - step):
            keep(at + 1, smooth(at, whole))
        finish(step - 1)
        finish(chunks - step)

    @pl.loop(2, last - 3)
    def _(step):
        tend(step)

    for side, turn in turns:
        @pl.when(relays & turn)
        def _():
            first_leg(side).wait_recv()
            second_leg(side).start()

    if lean:
        each(1, lambda peer: told(1, peer).wait_recv())
        total = far_flags[0]
        for peer in range(1, outer):
            total = total + far_flags[peer]
        flag[...] = total

    @pl.loop(last - 3, last - 1)
    def _(step):
        tend(step)

    @pl.when(has_up)
    def _():
        down.wait_recv()
        keep(0, edge_in[0])

    @pl.when(has_down)
    def _():
        up.wait_recv()
        keep(chunks + 1, edge_in[1])

    @pl.when(jnp.logical_not(has_up))
    def _():
        keep(0, jnp.zeros((size, width), F32))

    @pl.when(jnp.logical_not(has_down))
    def _():
        keep(chunks + 1, jnp.zeros((size, width), F32))

    finish(0)
    finish(chunks - 1)
    keep(last, smooth(last - 1, whole))
    ready = blend(1, own, last)
    for at in (last - 2, last + 1, last - 1, last):
        finish(at)

    arrive(last, whole)
    high, low = split(across(ready + blend(0, left_in, last, whole) + blend(2, right_in, last, whole)))
    three = 3 * size
    both = dot(tail_op[...], high)
    share = both[:three] + both[three:] + dot(tail_op[:three, :], low)
    for spot in range(3):
        out[last - 1 + spot] += share[spot * size:(spot + 1) * size]

    for side, turn in turns:
        @pl.when(relays & turn)
        def _():
            second_leg(side).wait_send()

    for (there, _), wait in zip(sides[2:], (up, down)):
        @pl.when(there)
        def _():
            wait.wait_send()

    if lean:
        for side in range(2):
            @pl.when(sides[side][0])
            def _():
                ask(side).wait_send()

        each(0, lambda peer: tell(0, peer).wait_send())
        each(1, lambda peer: tell(1, peer).wait_send())

    def sent(at, raw):
        @pl.when(has_right)
        def _():
            to_right(at, raw).wait_send()

        @pl.when(has_left)
        def _():
            to_left(at, raw).wait_send()

    sent(0, True)
    sent(chunks - 1, True)

    @pl.loop(1, chunks - 1)
    def _(at):
        sent(at, whole)


def store(x):
    pieces = 4

    def body(x_ref, out_ref, sem):
        step = x.shape[0] // pieces
        copies = [pltpu.make_async_copy(x_ref.at[pl.ds(at * step, step)], out_ref.at[pl.ds(at * step, step)], sem.at[at])
                  for at in range(pieces)]
        for copy in copies:
            copy.start()
        for copy in copies:
            copy.wait()

    return pl.pallas_call(
        body, out_shape=pltpu.HBM(x.shape, x.dtype), in_specs=[pl.BlockSpec(memory_space=pltpu.VMEM)],
        out_specs=pl.BlockSpec(memory_space=pltpu.HBM), scratch_shapes=[pltpu.SemaphoreType.DMA((pieces,))],
        compiler_params=pltpu.CompilerParams(vmem_limit_bytes=1 << 20), name="store",
    )(pltpu.with_memory_space_constraint(x, pltpu.VMEM))


def solution(mesh):
    groups, skies = mesh.shape["chan"], mesh.shape["sky"]

    def regrid(lean, cube, shifts, halfwidth, taps, beam_rows, beam_cols):
        chunks, size, width = cube.shape
        height, chans = chunks * BAND, size // BAND
        thin = SLOTS * BAND
        inner = min(INNER, groups)
        outer = groups // inner
        whole = (chunks, size, width)
        vmem = pl.BlockSpec(memory_space=pltpu.VMEM)
        results, extra = [pltpu.VMEM(whole, F32)], []
        if lean:
            results.append(jax.ShapeDtypeStruct((8, 128), F32))
            extra = [
                pltpu.VMEM((2, chans, 128), F32),
                pltpu.VMEM((2, chans, 128), F32),
                pltpu.VMEM((chunks, thin, width), F32),
                pltpu.VMEM((chunks, thin, width), F32),
                pltpu.VMEM((2, 2 * thin, 128), BF16),
                pltpu.VMEM((2, 2 * size, 128), BF16),
                pltpu.VMEM((inner, 8, 128), F32),
                pltpu.VMEM((outer, 8, 128), F32),
                pltpu.VMEM((2, 8, 128), F32),
                pltpu.SemaphoreType.DMA((2,)),
                pltpu.SemaphoreType.DMA((2,)),
                pltpu.SemaphoreType.DMA((2, max(inner, outer))),
                pltpu.SemaphoreType.DMA((2, max(inner, outer))),
            ]
        return pl.pallas_call(
            functools.partial(kernel, lean, groups, skies),
            out_shape=results,
            in_specs=[pl.BlockSpec(memory_space=pltpu.HBM)] * 6,
            out_specs=[vmem] * len(results),
            scratch_shapes=extra + [
                pltpu.SMEM(shifts.shape, jnp.int32),
                pltpu.SMEM(halfwidth.shape, jnp.int32),
                pltpu.VMEM(taps.shape, F32),
                pltpu.VMEM(whole, F32),
                pltpu.VMEM(whole, F32),
                pltpu.VMEM(whole, F32),
                pltpu.VMEM((chunks + 2, size, width), BF16),
                pltpu.VMEM((chunks + 2, size, width), BF16),
                pltpu.VMEM((6 * size, size), BF16),
                pltpu.VMEM((2, size, width), F32),
                pltpu.VMEM((2, size, width), F32),
                pltpu.VMEM((size, width), F32),
                pltpu.VMEM((width, width), F32),
                pltpu.VMEM((2, width, width), BF16),
                pltpu.VMEM((height, 3 * height), F32),
                pltpu.VMEM((chunks, 2 * size, 3 * size), BF16),
                pltpu.VMEM((2 * size, 3 * size), BF16),
                pltpu.SemaphoreType.DMA((8,)),
                pltpu.SemaphoreType.DMA((2, chunks)),
                pltpu.SemaphoreType.DMA((2, chunks)),
                pltpu.SemaphoreType.DMA((3,)),
                pltpu.SemaphoreType.DMA((3,)),
            ],
            compiler_params=pltpu.CompilerParams(
                collective_id=int(lean), has_side_effects=True, vmem_limit_bytes=40 << 20),
            name="regrid" if lean else "regrid_whole",
        )(*(pltpu.with_memory_space_constraint(x, pltpu.HBM) for x in (
            cube, shifts, halfwidth, taps, beam_rows, beam_cols)))

    def per_device(cube, *others):
        height, chans, width = cube.shape
        args = (cube.reshape(height // BAND, BAND * chans, width), *others)
        result, flag = regrid(True, *args)
        result, _ = lax.while_loop(
            lambda state: state[1] > 0.5,
            lambda state: (store(regrid(False, *args)[0]), jnp.zeros((), F32)),
            (store(result), flag[0, 0]))
        return result.reshape(cube.shape)

    return jax.shard_map(
        per_device,
        mesh=mesh,
        in_specs=(P("sky", "chan", None), P("chan"), P("chan"), P("chan", None), P(), P()),
        out_specs=P("sky", "chan", None),
        check_vma=False,
    )
```

time: 104 us -> 91 us (0.88)
  the two profiles are of different devices: /device:TPU:169 before, /device:TPU:32 now
where the time goes in v4:
time: 91 us; the launch traced here: 90.9 us
  Pallas kernels  89.4 us (98%)
    pallas_call x1, Pallas kernels, regrid(): pl.pallas_call(functools.partial(kernel, lean, groups, skies), out_shape=...  87.3 us
    pallas_call x1, Pallas kernels, store(): pl.pallas_call(body, out_shape=pltpu.HBM(x.shape, x.dtype), in_specs=[pl....  2.04 us

profile of v4, /device:TPU:32, one launch (start us, length us, event | category | flops | bytes accessed | tf_op | source)
XLA Modules:
  0.0 90.9 jit_solution(11724642727302916438)
XLA Ops:
  0.0 87.3 %regrid.1 = (f32[16,128,512]{2,1,0:T(8,128)S(1)}, f32[8,128]{1,0:T(8,128)S(1)}) custom-call(f32[16,128,512]{2,1,0:T(8,128)} %bitcast.3, s32[4]{0:T(128)} %refs_1_.1, s32[4]{0:T(128)} %refs_2_.1, f32[16,9]{1,0:T(8,128)} %refs_3_.1, f32[512,512]{1,0:T(8,128)} %refs_4_.1, f32[512,512]{1,0:T(8,128)} %refs_5_.1), custom_call_target="tpu_custom_call" | custom-call | tf_op jit(solution)/shard_map/regrid/pallas_call | solution.py:546
  87.3 0.6 slice.3
  87.9 2.0 %store.3 = f32[16,128,512]{2,1,0:T(8,128)} custom-call(f32[16,128,512]{2,1,0:T(8,128)S(1)} %get-tuple-element.47.x_ref), custom_call_target="tpu_custom_call" | custom-call | tf_op jit(solution)/shard_map/store/pallas_call | solution.py:510
  90.0 0.8 while.9

commit v5 on v4

--- a/solution.py
+++ b/solution.py
@@ -50,29 +50,40 @@
     shape = band.shape
     row, lane = iota(shape, 0), iota(shape, 1)
     ones, before = jnp.ones((128, 128), BF16), ones_where(iota((128, 128), 0) < iota((128, 128), 1))
+    one_rows = ones[:shape[0]]
     pattern = ones_where(band != 0.0)
     high, low = split(band)
-    touched = ones_where(dot_across(ones[:shape[0]], deepen(pattern)) > 0.5)
-    few_out = dot(touched, ones)
-    pick = ones_where((dot(touched, before).astype(jnp.int32) == row) & (touched > 0.5))
-    send_out = dot(pick, deepen(high)) + dot(pick, deepen(low))
-    touched = ones_where(dot(pattern, ones) > 0.5)
-    rank = dot(ones_where(lane < row), deepen(touched)).astype(jnp.int32)
-    receive_out = jnp.where((rank == lane) & (touched > 0.5), 1.0, 0.0)
-    touched = ones_where(dot(ones[:shape[0]], deepen(pattern)) > 0.5)
-    few_raw = dot(touched, ones)
-    pick = ones_where((dot(touched, before).astype(jnp.int32) == row) & (touched > 0.5))
-    outs = few_out <= few_raw
-    send = jnp.where(outs, send_out, pick.astype(F32))
-    high = jnp.where(outs, receive_out, dot_across(high, deepen(pick)))
-    low = jnp.where(outs, 0.0, dot_across(low, deepen(pick)))
-    return send, (high.astype(BF16), low.astype(BF16)), jnp.minimum(few_out, few_raw)
+    raw = jnp.zeros(shape, F32)
+    for block in range(shape[0] // BLK):
+        raw = jnp.where(lane // BLK == block, (row // 2 ** block % 2).astype(F32), raw)
+    touched = jnp.where(dot_across(one_rows, deepen(pattern)) > 0.5, 1.0, 0.0)
+    channels = ones_where(dot(raw.astype(BF16), deepen(pattern)) > 0.5)
+    cost = dot(channels, ones) + dot((touched * (1.0 - raw)).astype(BF16), ones)
+    score = cost * shape[0] + row.astype(F32)
+    best = jnp.min(score, axis=0, keepdims=True)
+    chosen = jnp.sum(jnp.where(score == best, raw, 0.0), axis=0, keepdims=True)
+    raw = dot(ones_where((row == lane) & (chosen > 0.5)), ones)
+    pattern_raw = (pattern.astype(F32) * raw).astype(BF16)
+    pattern_out = (pattern.astype(F32) * (1.0 - raw)).astype(BF16)
+    hit = ones_where(dot(one_rows, deepen(pattern_raw)) > 0.5)
+    channels = dot(hit, ones)
+    pick_raw = ones_where((dot(hit, before) == row.astype(F32)) & (hit > 0.5))
+    hit = ones_where(dot_across(one_rows, deepen(pattern_out)) > 0.5)
+    count = channels + dot(hit, ones)
+    pick_out = ones_where((channels + dot(hit, before) == row.astype(F32)) & (hit > 0.5))
+    send = pick_raw.astype(F32) + (dot(pick_out, deepen(high)) + dot(pick_out, deepen(low)))
+    hit = ones_where(dot(pattern_out, ones) > 0.5)
+    place = channels + dot(ones_where(lane < row), deepen(hit))
+    receive_out = jnp.where((place == lane.astype(F32)) & (hit > 0.5), 1.0, 0.0)
+    high_raw = dot_across((high.astype(F32) * raw).astype(BF16), deepen(pick_raw))
+    low_raw = dot_across((low.astype(F32) * raw).astype(BF16), deepen(pick_raw))
+    return send, ((receive_out + high_raw).astype(BF16), low_raw.astype(BF16)), count
 
 
 def kernel(lean, groups, skies, *refs):
     cube, shifts_in, halfwidth_in, taps_in, beam_rows, beam_cols, out, *refs = refs
     if lean:
-        flag, needs, asked, for_left, for_right, send_ops, receive_ops, near_flags, far_flags, my_flag, *refs = refs
+        flag, needs, asked, for_both, send_op, receive_ops, near_flags, far_flags, my_flag, *refs = refs
         need_send, need_recv, flag_send, flag_recv, *refs = refs
     (shifts, halfwidth, taps, own, left_in, right_in, spread, spread_low, tail_op, edge_out, edge_in, detour, cols,
      cols_pair, rows, row_ops, chan_op, local_sem, send_sem, recv_sem, edge_send, edge_recv) = refs
@@ -179,25 +190,28 @@
 
     def to_right(at, raw):
         return pltpu.make_async_remote_copy(
-            src_ref=cube.at[at] if raw else for_right.at[at], dst_ref=thinned(left_in, at, raw),
+            src_ref=cube.at[at] if raw else for_both.at[at, pl.ds(thin, thin)], dst_ref=thinned(left_in, at, raw),
             send_sem=send_sem.at[0, at], recv_sem=recv_sem.at[0, at],
             device_id={"chan": group + 1}, device_id_type=MESH)
 
     def to_left(at, raw):
         return pltpu.make_async_remote_copy(
-            src_ref=cube.at[at] if raw else for_left.at[at], dst_ref=thinned(right_in, at, raw),
+            src_ref=cube.at[at] if raw else for_both.at[at, pl.ds(0, thin)], dst_ref=thinned(right_in, at, raw),
             send_sem=send_sem.at[1, at], recv_sem=recv_sem.at[1, at],
             device_id={"chan": group - 1}, device_id_type=MESH)
 
-    def send(step, raw):
-        for at in (step, chunks - 1 - step):
-            @pl.when(has_right)
-            def _():
-                to_right(at, raw).start()
-
-            @pl.when(has_left)
-            def _():
-                to_left(at, raw).start()
+    def send(at, raw):
+        @pl.when(has_right)
+        def _():
+            to_right(at, raw).start()
+
+        @pl.when(has_left)
+        def _():
+            to_left(at, raw).start()
+
+    def send_pair(step, raw):
+        send(step, raw)
+        send(chunks - 1 - step, raw)
 
     def ask(side):
         return pltpu.make_async_remote_copy(
@@ -232,7 +246,8 @@
 
     send(0, True)
     if not lean:
-        send(1, True)
+        send(chunks - 1, True)
+        send_pair(1, True)
 
     @pl.when(jnp.logical_not(has_left))
     def _():
@@ -250,24 +265,8 @@
         both = dot(op, high)
         return both[:rows_out] + both[rows_out:] + dot(op[:rows_out], low)
 
-    def reduce_for(step):
-        for at in (step, chunks - 1 - step):
-            for side, ref in enumerate((for_left, for_right)):
-                ref[at] = apply(send_ops[side], own[at], thin)
-
-    if lean:
-        for side in range(2):
-            @pl.when(sides[side][0])
-            def _():
-                ask(1 - side).wait_recv()
-
-        pick = ones_where(iota((128, 128), 0) == iota((128, 128), 1) % chans)
-        same_row = iota((128, 128), 0) % BAND == iota((128, 128), 1) // chans
-        for side in range(2):
-            for half, part in enumerate(split(asked[side])):
-                wide = jnp.broadcast_to(dot(part, pick)[:, None, :], (chans, BAND, 128)).reshape(128, 128)
-                send_ops[side, pl.ds(half * thin, thin), :] = jnp.where(same_row, wide, 0.0)[:thin].astype(BF16)
-        reduce_for(1)
+    def reduce_for(at):
+        for_both[at] = apply(send_op[...], own[at], 2 * thin)
 
     pick = ones_where(iota((128, size), 0) == iota((128, size), 1) % chans)
     same_row = iota((size, size), 0) // chans == iota((size, size), 1) // chans
@@ -276,14 +275,29 @@
             wide = jnp.concatenate([dot(part, pick)] * BAND, axis=0)
             chan_op[pl.ds(half * size, size), pl.ds(slot * size, size)] = jnp.where(same_row, wide, 0.0).astype(BF16)
     if lean:
-        send(1, False)
         pick = ones_where(iota((128, 128), 0) == iota((128, 128), 1) // BAND)
         same_row = iota((size, 128), 0) // chans == iota((size, 128), 1) % BAND
         for side, receive in enumerate(receives):
             for half, part in enumerate(receive):
                 wide = jnp.concatenate([dot(part, pick)] * BAND, axis=0)
                 receive_ops[side, pl.ds(half * size, size), :] = jnp.where(same_row, wide, 0.0).astype(BF16)
-        reduce_for(2)
+
+        for side in range(2):
+            @pl.when(sides[side][0])
+            def _():
+                ask(1 - side).wait_recv()
+
+        pick = ones_where(iota((128, 128), 0) == iota((128, 128), 1) % chans)
+        same_row = iota((128, 128), 0) % BAND == iota((128, 128), 1) // chans
+        for side in range(2):
+            for half, part in enumerate(split(asked[side])):
+                wide = jnp.broadcast_to(dot(part, pick)[:, None, :], (chans, BAND, 128)).reshape(128, 128)
+                send_op[pl.ds((2 * half + side) * thin, thin), :] = jnp.where(same_row, wide, 0.0)[:thin].astype(BF16)
+        reduce_for(chunks - 1)
+        reduce_for(1)
+        send(chunks - 1, False)
+        reduce_for(chunks - 2)
+        send(1, False)
 
     high, low = split(cols[...])
     cols_pair[0] = high
@@ -300,6 +314,10 @@
             wide = jnp.broadcast_to(wide[:, None, :], (BAND, chans, 3 * size)).reshape(size, 3 * size)
             row_ops[at, pl.ds(half * size, size), :] = jnp.where(same_chan, wide, 0.0).astype(BF16)
 
+    if lean:
+        reduce_for(2)
+        send(chunks - 2, False)
+
     def keep(at, value):
         high, low = split(value)
         spread[at] = high
@@ -335,9 +353,12 @@
 
     whole = not lean
     for side, at in enumerate((0, chunks - 1)):
-        value = smooth(at, True)
+        value = smooth(at, at == 0 or whole)
         edge_out[side] = value
         keep(at + 1, value)
+        if lean:
+            reduce_for((chunks - 3, 3)[side])
+            send((2, chunks - 3)[side], False)
     if lean:
         each(0, lambda peer: told(0, peer).wait_recv())
         total = near_flags[0]
@@ -375,14 +396,25 @@
         def _():
             first_leg(side).start()
 
-    for step in range(2, AHEAD + 2):
-        send(step, whole)
-        if lean:
-            reduce_for(step + 1)
-    for at in (1, chunks - 2):
-        keep(at + 1, smooth(at, whole))
     if lean:
         each(1, lambda peer: tell(1, peer).start())
+
+        @pl.loop(3, last)
+        def _(step):
+            reduce_for(chunks - 1 - step)
+            send(step, False)
+
+            @pl.when(step < last - 1)
+            def _():
+                reduce_for(step + 1)
+                send(chunks - 1 - step, False)
+    else:
+        for step in range(2, AHEAD + 2):
+            send_pair(step, True)
+    keep(2, smooth(1, whole))
+    if lean:
+        send(last, False)
+    keep(chunks - 1, smooth(chunks - 2, whole))
 
     keep(last + 1, jnp.zeros((size, width), F32))
     for spot in range(3):
@@ -391,14 +423,10 @@
                 last - 1 + spot, pl.ds(half * size, size), (2 - spot) * size:(3 - spot) * size]
 
     def tend(step):
-        @pl.when(step + AHEAD < last)
-        def _():
-            send(step + AHEAD, whole)
-
-        if lean:
-            @pl.when(step + AHEAD + 1 < last)
+        if not lean:
+            @pl.when(step + AHEAD < last)
             def _():
-                reduce_for(step + AHEAD + 1)
+                send_pair(step + AHEAD, True)
 
         for at in (step, chunks - 1 - step):
             keep(at + 1, smooth(at, whole))
@@ -415,38 +443,38 @@
             first_leg(side).wait_recv()
             second_leg(side).start()
 
+    @pl.loop(last - 3, last - 1)
+    def _(step):
+        tend(step)
+
+    @pl.when(has_up)
+    def _():
+        down.wait_recv()
+        keep(0, edge_in[0])
+
+    @pl.when(has_down)
+    def _():
+        up.wait_recv()
+        keep(chunks + 1, edge_in[1])
+
+    @pl.when(jnp.logical_not(has_up))
+    def _():
+        keep(0, jnp.zeros((size, width), F32))
+
+    @pl.when(jnp.logical_not(has_down))
+    def _():
+        keep(chunks + 1, jnp.zeros((size, width), F32))
+
+    finish(0)
+    finish(chunks - 1)
+    keep(last, smooth(last - 1, whole))
     if lean:
         each(1, lambda peer: told(1, peer).wait_recv())
         total = far_flags[0]
         for peer in range(1, outer):
             total = total + far_flags[peer]
-        flag[...] = total
-
-    @pl.loop(last - 3, last - 1)
-    def _(step):
-        tend(step)
-
-    @pl.when(has_up)
-    def _():
-        down.wait_recv()
-        keep(0, edge_in[0])
-
-    @pl.when(has_down)
-    def _():
-        up.wait_recv()
-        keep(chunks + 1, edge_in[1])
-
-    @pl.when(jnp.logical_not(has_up))
-    def _():
-        keep(0, jnp.zeros((size, width), F32))
-
-    @pl.when(jnp.logical_not(has_down))
-    def _():
-        keep(chunks + 1, jnp.zeros((size, width), F32))
-
-    finish(0)
-    finish(chunks - 1)
-    keep(last, smooth(last - 1, whole))
+        flag[...] = total[:1, :1]
+
     ready = blend(1, own, last)
     for at in (last - 2, last + 1, last - 1, last):
         finish(at)
@@ -488,9 +516,8 @@
             to_left(at, raw).wait_send()
 
     sent(0, True)
-    sent(chunks - 1, True)
-
-    @pl.loop(1, chunks - 1)
+
+    @pl.loop(1, chunks)
     def _(at):
         sent(at, whole)
 
@@ -527,13 +554,12 @@
         vmem = pl.BlockSpec(memory_space=pltpu.VMEM)
         results, extra = [pltpu.VMEM(whole, F32)], []
         if lean:
-            results.append(jax.ShapeDtypeStruct((8, 128), F32))
+            results.append(jax.ShapeDtypeStruct((1, 1), F32))
             extra = [
                 pltpu.VMEM((2, chans, 128), F32),
                 pltpu.VMEM((2, chans, 128), F32),
-                pltpu.VMEM((chunks, thin, width), F32),
-                pltpu.VMEM((chunks, thin, width), F32),
-                pltpu.VMEM((2, 2 * thin, 128), BF16),
+                pltpu.VMEM((chunks, 2 * thin, width), F32),
+                pltpu.VMEM((4 * thin, 128), BF16),
                 pltpu.VMEM((2, 2 * size, 128), BF16),
                 pltpu.VMEM((inner, 8, 128), F32),
                 pltpu.VMEM((outer, 8, 128), F32),

time: 91 us -> 88.5 us (0.973)
  the two profiles are of different devices: /device:TPU:32 before, /device:TPU:1 now
where the time goes in v5:
time: 88.5 us; the launch traced here: 87.4 us
  Pallas kernels  86.4 us (98%)
    pallas_call x1, Pallas kernels, regrid(): pl.pallas_call(functools.partial(kernel, lean, groups, skies), out_shape=...  84.4 us
    pallas_call x1, Pallas kernels, store(): pl.pallas_call(body, out_shape=pltpu.HBM(x.shape, x.dtype), in_specs=[pl....  2.04 us

profile of v5, /device:TPU:1, one launch (start us, length us, event | category | flops | bytes accessed | tf_op | source)
XLA Modules:
  0.0 87.4 jit_solution(3570621000510605625)
XLA Ops:
  0.0 84.4 %regrid.1 = (f32[16,128,512]{2,1,0:T(8,128)S(1)}, f32[1,1]{1,0:T(1,128)}) custom-call(f32[16,128,512]{2,1,0:T(8,128)} %bitcast.3, s32[4]{0:T(128)} %refs_1_.1, s32[4]{0:T(128)} %refs_2_.1, f32[16,9]{1,0:T(8,128)} %refs_3_.1, f32[512,512]{1,0:T(8,128)} %refs_4_.1, f32[512,512]{1,0:T(8,128)} %refs_5_.1), custom_call_target="tpu_custom_call" | custom-call | tf_op jit(solution)/shard_map/regrid/pallas_call | solution.py:572
  84.4 2.0 %store.3 = f32[16,128,512]{2,1,0:T(8,128)} custom-call(f32[16,128,512]{2,1,0:T(8,128)S(1)} %get-tuple-element.47.x_ref), custom_call_target="tpu_custom_call" | custom-call | tf_op jit(solution)/shard_map/store/pallas_call | solution.py:537
  86.4 0.8 while.9
